TPU v7x, 32 devices: a whole 2x2x4 slice. The times are simulated.
32 devices in a mesh: section: 8 (over y, x, core), tensor: 4 (over z).
Axes of the slice: x: 2, y: 2, z: 4, core: 2. Of those that a mesh axis runs over, the one named last changes fastest.
Arguments:
- acts: bfloat16 [8, 2, 32, 4096], P('section', None, None, 'tensor'), may hold values from -6 to 6
- grads_in: bfloat16 [8, 2, 32, 4096], P('section', None, None, 'tensor'), may hold values from -6 to 6
- head_grads: bfloat16 [8, 2, 128, 512], P('section', None, None, 'tensor'), may hold values from -6 to 6
- types: int32 [8, 2, 32], P('section'), may hold values 0 or 1
- gains: bfloat16 [8, 2, 2, 1024], P('section'), may hold values from 0.3984375 to 1.59375
- w_query: bfloat16 [8, 2, 4096, 512], P('section', None, None, 'tensor'), may hold values from -0.09375 to 0.09375
- w_key: bfloat16 [8, 2, 4096, 128], P('section', None, None, 'tensor'), may hold values from -0.09375 to 0.09375
- w_value: bfloat16 [8, 2, 4096, 128], P('section', None, None, 'tensor'), may hold values from -0.09375 to 0.09375
Outputs:
- routed: bfloat16 [8, 2, 32, 4096], P('section', None, None, 'tensor')
All inputs are finite; a program needn't handle non-finite values. No bound on the sum of `types` on one device may be relied on, other than what follows from the above.
Results may differ from a plain program's by a relative error of at most 0.0055.
Values may be sent and summed in bfloat16 or wider, within the bound.
A program may use at most 64 MiB of HBM per device.

v0:
```python
import jax
import jax.numpy as jnp
from jax import lax
from jax.sharding import PartitionSpec as P

HEAD_DIM = 128
SUB = 4
epsilon = 1e-05


def swapped(value, axis, stride):
    mask = 2**stride
    pairs = [(source, source ^ mask) for source in range(lax.axis_size(axis))]
    return lax.ppermute(value, axis, pairs)


def shifted(value, axis, by):
    peers = lax.axis_size(axis)
    return lax.ppermute(value, axis, [(i, (i + by) % peers) for i in range(peers)])


def sum_columns(first, second):
    return (
        lax.psum_scatter(first, "tensor", scatter_dimension=2, tiled=True),
        lax.psum_scatter(second, "tensor", scatter_dimension=2, tiled=True),
    )


def collect_rows(member, position, levels, axis):
    for bit in range(levels):
        partner = swapped(member, "section", bit)
        upper_bit = position >> bit & 1
        member = jnp.where(
            upper_bit == 1,
            jnp.concatenate([partner, member], axis=axis),
            jnp.concatenate([member, partner], axis=axis),
        )
    return member


def halve_once(member, upper_bit, bit):
    half_rows = member.shape[1] // 2
    lower_rows = member[:, :half_rows]
    higher_rows = member[:, half_rows:]
    kept_rows = jnp.where(upper_bit == 1, higher_rows, lower_rows)
    sent_rows = jnp.where(upper_bit == 1, lower_rows, higher_rows)
    return kept_rows + swapped(sent_rows, "section", bit)


def reduce_rows(first, second, position, levels):
    for bit in reversed(range(levels)):
        upper_bit = position >> bit & 1
        first = halve_once(first, upper_bit, bit)
        second = halve_once(second, upper_bit, bit)
    return (first, second)


def per_device(acts, grads_in, head_grads, types, gains, w_query, w_key, w_value):
    tensors = lax.axis_size("tensor")
    section_count = lax.axis_size("section") // SUB
    levels = SUB.bit_length() - 1
    position = lax.axis_index("section") % SUB
    section_here = lax.axis_index("section") // SUB
    x_local = acts[0]
    grad_local = grads_in[0]
    out_grads = head_grads[0]
    w_query = w_query[0]
    w_key = w_key[0]
    w_value = w_value[0]
    x_cols = lax.all_gather(x_local, "tensor", axis=2, tiled=True)
    x_full = collect_rows(x_cols, position, levels, 1)
    kind_full = collect_rows(types[0].astype(jnp.bfloat16), position, levels, 1)
    gain_full = collect_rows(gains[0], position, levels, 2).astype(jnp.float32)
    tokens = x_full.shape[1]
    tokq = x_local.shape[1]
    width = x_full.shape[2]
    cols_dev = x_local.shape[2]
    x_float = x_full.astype(jnp.float32)
    inverse = lax.rsqrt(jnp.mean(x_float * x_float, axis=-1, keepdims=True) + epsilon)
    gain_rows = jnp.where(kind_full[..., None] > 0.5, gain_full[:, 1:2, :], gain_full[:, 0:1, :])
    normed = (x_float * inverse * gain_rows).astype(jnp.bfloat16)
    queries = jnp.einsum(
        "ctd,cdh->cth", normed, w_query, preferred_element_type=jnp.float32
    ).astype(jnp.bfloat16)
    key_part = jnp.einsum("ctd,cdh->cth", normed, w_key, preferred_element_type=jnp.float32).astype(
        jnp.bfloat16
    )
    value_part = jnp.einsum(
        "ctd,cdh->cth", normed, w_value, preferred_element_type=jnp.float32
    ).astype(jnp.bfloat16)
    key_rows, value_rows = (
        lax.all_gather(key_part, "tensor", axis=2, tiled=True),
        lax.all_gather(value_part, "tensor", axis=2, tiled=True),
    )
    softmax_scale = HEAD_DIM ** (-0.5)
    scores = (
        jnp.einsum("cqh,ckh->cqk", queries, key_rows, preferred_element_type=jnp.float32)
        * softmax_scale
    )
    causal = jnp.arange(tokens)[:, None] >= jnp.arange(tokens)[None, :]
    scores = jnp.where(causal[None], scores, -1e30)
    attn_probs = jax.nn.softmax(scores, axis=-1)
    probs_low = attn_probs.astype(jnp.bfloat16)
    prob_grads = jnp.einsum(
        "cqh,ckh->cqk", out_grads, value_rows, preferred_element_type=jnp.float32
    )
    score_grads = (
        attn_probs
        * (prob_grads - jnp.sum(prob_grads * attn_probs, axis=-1, keepdims=True))
        * softmax_scale
    ).astype(jnp.bfloat16)
    query_grads = jnp.einsum(
        "cqk,ckh->cqh", score_grads, key_rows, preferred_element_type=jnp.float32
    ).astype(jnp.bfloat16)
    key_each = jnp.einsum("cqk,cqh->ckh", score_grads, queries, preferred_element_type=jnp.float32)
    value_each = jnp.einsum(
        "cqk,cqh->ckh", probs_low, out_grads, preferred_element_type=jnp.float32
    )
    key_sum, value_sum = sum_columns(key_each, value_each)
    key_grads = key_sum.astype(jnp.bfloat16)
    value_grads = value_sum.astype(jnp.bfloat16)
    joined_grads = jnp.concatenate([query_grads, key_grads, value_grads], axis=2)
    joined_weights = jnp.concatenate([w_query, w_key, w_value], axis=2)
    partial_value = jnp.einsum(
        "cth,cdh->ctd", joined_grads, joined_weights, preferred_element_type=jnp.float32
    )
    stat_part = jnp.sum(x_float * gain_rows * partial_value, axis=-1)
    stat_wide = jnp.broadcast_to(stat_part[..., None], stat_part.shape + (tensors,))
    grad_rows_sum, stat_rows = reduce_rows(partial_value, stat_wide, position, levels)
    grad_mine, stat_mine = sum_columns(grad_rows_sum, stat_rows)
    my_inverse = lax.dynamic_slice_in_dim(inverse, position * tokq, tokq, 1)
    my_gain = lax.dynamic_slice_in_dim(gain_rows, position * tokq, tokq, 1)
    my_gain = lax.dynamic_slice_in_dim(my_gain, lax.axis_index("tensor") * cols_dev, cols_dev, 2)
    my_x = x_local.astype(jnp.float32)
    stat_mean = stat_mine / width
    norm_grads = my_inverse * my_gain * grad_mine - my_x * my_inverse**3 * stat_mean
    result = (grad_local.astype(jnp.float32) + norm_grads).astype(jnp.bfloat16)
    arrived = shifted(result, "section", -SUB)
    routed = jnp.where(section_here == section_count - 1, arrived[::-1], arrived)
    return routed[None]


def solution(mesh):
    return jax.shard_map(
        per_device,
        mesh=mesh,
        in_specs=(
            P("section", None, None, "tensor"),
            P("section", None, None, "tensor"),
            P("section", None, None, "tensor"),
            P("section", None, None),
            P("section", None, None, None),
            P("section", None, None, "tensor"),
            P("section", None, None, "tensor"),
            P("section", None, None, "tensor"),
        ),
        out_specs=P("section", None, None, "tensor"),
        check_vma=False,
    )
```

profile of v0, /device:TPU:0, one launch (start us, length us, event | category | flops | bytes accessed | tf_op | source)
XLA Modules:
  0.0 225.5 jit_solution(11091461946398277763)
XLA Ops:
  6.5 0.7 convert_bitcast_fusion
  7.3 0.5 collective-permute-start.2
  7.8 17.7 %all-gather = bf16[1,2,32,4096]{3,2,1,0:T(8,128)(2,1)S(1)} all-gather(bf16[1,2,32,1024]{3,2,1,0:T(8,128)(2,1)} %param.8), channel_id=2, replica_groups=mesh['section'=8,'tensor'=4] {'tensor'}, dimensions={3}, use_global_device_ids=true | all-gather | bytes 655360 | tf_op jit(solution)/shard_map/all_gather | solution.py:70
  25.6 1.5 collective-permute-start.3
  27.1 0.8 broadcast_select_fusion.2
  27.9 0.6 collective-permute-start.5
  28.5 0.7 collective-permute-done.3
  29.2 0.1 fusion.52
  29.2 2.4 %collective-permute-done.5 = bf16[2,2,2048]{2,1,0:T(2,128)(2,1)S(1)} collective-permute-done((bf16[2,2,2048]{2,1,0:T(2,128)(2,1)S(1)}, bf16[2,2,2048]{2,1,0:T(2,128)(2,1)S(1)}, u32[]{:S(2)}, u32[]{:S(2)}) %collective-permute-start.5) | collective-permute-done | bytes 16416 | tf_op jit(solution)/shard_map/ppermute | solution.py:14
  31.7 0.2 maximum_select_fusion.1
  32.0 0.6 collective-permute-start.1
  32.7 23.5 %collective-permute-done.1 = bf16[2,64,4096]{2,1,0:T(8,128)(2,1)S(1)} collective-permute-done((bf16[2,64,4096]{2,1,0:T(8,128)(2,1)S(1)}, bf16[2,64,4096]{2,1,0:T(8,128)(2,1)S(1)}, u32[]{:S(2)}, u32[]{:S(2)}) %collective-permute-start.1) | collective-permute-done | bytes 1048608 | tf_op jit(solution)/shard_map/ppermute | solution.py:14
  56.2 0.8 fusion.2
  57.0 1.3 convolution_convert_fusion.2
  58.2 13.4 %all_gather.10 = bf16[2,128,128]{1,2,0:T(8,128)(2,1)S(1)} all-gather(bf16[2,128,32]{1,2,0:T(8,128)(2,1)S(1)} %convolution_convert_fusion.2), channel_id=1, replica_groups=mesh['section'=8,'tensor'=4] {'tensor'}, dimensions={2}, use_global_device_ids=true | all-gather | bytes 81920 | tf_op jit(solution)/shard_map/all_gather | solution.py:92
  71.7 1.3 convolution_convert_fusion.1
  72.9 13.2 %all_gather.11 = bf16[2,128,128]{1,2,0:T(8,128)(2,1)S(1)} all-gather(bf16[2,128,32]{1,2,0:T(8,128)(2,1)S(1)} %convolution_convert_fusion.1), channel_id=1, replica_groups=mesh['section'=8,'tensor'=4] {'tensor'}, dimensions={2}, use_global_device_ids=true | all-gather | bytes 81920 | tf_op jit(solution)/shard_map/all_gather | solution.py:93
  86.2 1.4 fusion.22
  87.5 0.2 fusion.18
  87.8 0.7 fusion.61
  88.5 0.9 fusion.43
  89.4 0.2 convolution_bitcast_fusion
  89.6 1.9 fusion.25
  91.6 2.8 %copy.11 = bf16[1,2,4096,128]{2,3,1,0:T(8,128)(2,1)} copy(bf16[1,2,4096,128]{3,2,1,0:T(8,128)(2,1)S(1)} %copy-done.1) | data formatting | bytes 4194304 | tf_op args[5]
  94.4 1.2 convolution_convert_fusion
  95.6 13.9 %reduce-scatter.6.cloned.1.call-done = f32[2,128,32]{1,2,0:T(8,128)} async-done(((f32[2,128,128]{1,2,0:T(8,128)}), f32[2,128,32]{1,2,0:T(8,128)}) %reduce-scatter.6.cloned.1.call-update) | async-done | bytes 32784 | tf_op jit(solution)/shard_map/reduce_scatter | solution.py:25
  109.5 0.8 convert_element_type.65
  110.2 19.1 %reduce-scatter.4.cloned.1.call-done = f32[2,128,32]{1,2,0:T(8,128)} async-done(((f32[2,128,128]{1,2,0:T(8,128)}), f32[2,128,32]{1,2,0:T(8,128)}) %reduce-scatter.4.cloned.1.call-update) | async-done | bytes 32784 | tf_op jit(solution)/shard_map/reduce_scatter | solution.py:24
  129.4 0.8 convert_element_type.63
  130.1 5.5 %fusion.6 = (f32[2,128]{1,0:T(2,128)S(1)}, f32[2,128,4096]{2,1,0:T(8,128)}, f32[2,128,4096]{2,1,0:T(8,128)S(1)}) fusion(f32[2,4096]{1,0:T(2,128)S(1)} %copy-done.6, f32[2,4096]{1,0:T(2,128)S(1)} %copy-done.8, pred[2,128]{1,0:T(4,128)(4,1)} %copy-done.11, bf16[2,64,4096]{2,1,0:T(8,128)(2,1)} %copy-done.2, bf16[2,64,4096]{2,1,0:T(8,128)(2,1)S(1)} %maximum_select_fusion.1, ...), kind=kOutput, calls=%fused_computation.9 | convolution fusion | flops 427065088 | bytes 13796609 | tf_op jit(solution)/shard_map/cth,cdh->ctd/dot_general | solution.py:124
  135.7 0.3 slice_select_fusion
  135.9 1.5 collective-permute-start.6
  137.5 43.5 %collective-permute-done.6 = f32[2,64,4096]{2,1,0:T(8,128)S(1)} collective-permute-done((f32[2,64,4096]{2,1,0:T(8,128)S(1)}, f32[2,64,4096]{2,1,0:T(8,128)S(1)}, u32[]{:S(2)}, u32[]{:S(2)}) %collective-permute-start.6) | collective-permute-done | bytes 2097184 | tf_op jit(solution)/shard_map/ppermute | solution.py:14
  181.0 0.4 select_add_fusion
  181.4 0.1 slice_select_fusion.1
  181.7 2.6 %collective-permute-done.7 = f32[2,32,4096]{2,1,0:T(8,128)S(1)} collective-permute-done((f32[2,32,4096]{2,1,0:T(8,128)S(1)}, f32[2,32,4096]{2,1,0:T(8,128)S(1)}, u32[]{:S(2)}, u32[]{:S(2)}) %collective-permute-start.7) | collective-permute-done | bytes 1048608 | tf_op jit(solution)/shard_map/ppermute | solution.py:14
  184.3 1.2 select_add_fusion.1
  185.6 1.5 collective-permute-start.8
  187.1 0.6 dynamic-slice.4
  187.7 1.6 collective-permute-done.8
  189.4 1.1 collective-permute-done.9
  190.6 10.0 %all-reduce = f32[2,32,4]{1,0,2:T(2,128)S(1)} all-reduce(f32[2,32,4]{1,0,2:T(2,128)S(1)} %select_add_fusion.2), channel_id=6, replica_groups=mesh['section'=8,'tensor'=4] {'tensor'}, use_global_device_ids=true, to_apply=%region_8.9.clone | all-reduce | flops 256 | bytes 2048
  200.6 0.7 fusion.51
  201.2 10.7 %reduce-scatter.8.cloned.1.call-done = f32[2,32,1024]{2,1,0:T(8,128)} async-done(((f32[2,32,4096]{2,1,0:T(8,128)}), f32[2,32,1024]{2,1,0:T(8,128)}) %reduce-scatter.8.cloned.1.call-update) | async-done | bytes 262160 | tf_op jit(solution)/shard_map/reduce_scatter | solution.py:24
  212.0 1.2 fusion.32
  213.2 1.5 collective-permute-start.10
  214.8 3.5 %collective-permute-done.10 = bf16[2,32,1024]{2,1,0:T(8,128)(2,1)S(1)} collective-permute-done((bf16[2,32,1024]{2,1,0:T(8,128)(2,1)S(1)}, bf16[2,32,1024]{2,1,0:T(8,128)(2,1)S(1)}, u32[]{:S(2)}, u32[]{:S(2)}) %collective-permute-start.10) | collective-permute-done | bytes 131104 | tf_op jit(solution)/shard_map/ppermute | solution.py:19
  218.3 0.7 fusion.37
  (56 shorter events, 0.9 us)
Async XLA Ops:
  6.5 81.9 %copy-start = (bf16[1,2,128,128]{3,2,1,0:T(8,128)(2,1)S(1)}, bf16[1,2,128,128]{3,2,1,0:T(8,128)(2,1)}, u32[]{:S(2)}) copy-start(bf16[1,2,128,128]{3,2,1,0:T(8,128)(2,1)} %param.10) | copy-start | bytes 196612
  6.5 50.4 %copy-start.12 = (bf16[1,2,4096,32]{2,3,1,0:T(8,128)(2,1)S(1)}, bf16[1,2,4096,32]{2,3,1,0:T(8,128)(2,1)}, u32[]{:S(2)}) copy-start(bf16[1,2,4096,32]{2,3,1,0:T(8,128)(2,1)} %param.14) | copy-start | bytes 1572868
  6.5 102.9 %reduce-scatter.6.cloned.1.call-start = ((), (), s32[]{:S(2)}) async-start(), calls=%async_computation.4 | async-start | bytes 163840 | tf_op jit(solution)/shard_map/reduce_scatter | solution.py:25
  7.3 18.2 %collective-permute-start.2 = (bf16[2,32]{1,0:T(2,128)(2,1)S(1)}, bf16[2,32]{1,0:T(2,128)(2,1)S(1)}, u32[]{:S(2)}, u32[]{:S(2)}) collective-permute-start(bf16[2,32]{1,0:T(2,128)(2,1)S(1)} %convert_bitcast_fusion), channel_id=1, source_target_pairs={{0,4},{4,0},{8,12},{12,8},{16,20},{20,16},{24,28},{28,24},{1,5},{5... | collective-permute-start | bytes 392 | tf_op jit(solution)/shard_map/ppermute | solution.py:14
  7.8 19.3 %collective-permute-start.4 = (bf16[2,2,1024]{2,1,0:T(2,128)(2,1)}, bf16[2,2,1024]{2,1,0:T(2,128)(2,1)S(1)}, u32[]{:S(2)}, u32[]{:S(2)}) collective-permute-start(bf16[2,2,1024]{2,1,0:T(2,128)(2,1)} %bitcast.58), channel_id=1, source_target_pairs={{0,4},{4,0},{8,12},{12,8},{16,20},{20,16},{24,28},{28,24},{1,5},{5... | collective-permute-start | bytes 24584 | tf_op jit(solution)/shard_map/ppermute | solution.py:14
  25.5 6.3 %collective-permute-start = (bf16[2,32,4096]{2,1,0:T(8,128)(2,1)S(1)}, bf16[2,32,4096]{2,1,0:T(8,128)(2,1)S(1)}, u32[]{:S(2)}, u32[]{:S(2)}) collective-permute-start(bf16[2,32,4096]{2,1,0:T(8,128)(2,1)S(1)} %bitcast.52), channel_id=1, source_target_pairs={{0,4},{4,0},{8,12},{12,8},{16,20},{20,16},{24,28},{28,24},{1,5},{5... | collective-permute-start | bytes 1572872 | tf_op jit(solution)/shard_map/ppermute | solution.py:14
  25.6 3.6 %collective-permute-start.3 = (bf16[2,64]{1,0:T(2,128)(2,1)S(1)}, bf16[2,64]{1,0:T(2,128)(2,1)S(1)}, u32[]{:S(2)}, u32[]{:S(2)}) collective-permute-start(bf16[2,64]{1,0:T(2,128)(2,1)S(1)} %broadcast_select_fusion.6), channel_id=1, source_target_pairs={{0,8},{4,12},{8,0},{12,4},{16,24},{20,28},{24,16},{28,20},{1,9},{5... | collective-permute-start | bytes 776 | tf_op jit(solution)/shard_map/ppermute | solution.py:14
  27.9 3.8 %collective-permute-start.5 = (bf16[2,2,2048]{2,1,0:T(2,128)(2,1)S(1)}, bf16[2,2,2048]{2,1,0:T(2,128)(2,1)S(1)}, u32[]{:S(2)}, u32[]{:S(2)}) collective-permute-start(bf16[2,2,2048]{2,1,0:T(2,128)(2,1)S(1)} %broadcast_select_fusion.2), channel_id=1, source_target_pairs={{0,8},{4,12},{8,0},{12,4},{16,24},{20,28},{24,16},{28,20},{1,9},{5... | collective-permute-start | bytes 49160 | tf_op jit(solution)/shard_map/ppermute | solution.py:14
  29.2 56.9 %copy-start.11 = (pred[2,128]{1,0:T(4,128)(4,1)}, pred[2,128]{1,0:T(4,128)(4,1)S(1)}, u32[]{:S(2)}) copy-start(pred[2,128]{1,0:T(4,128)(4,1)S(1)} %fusion.52) | copy-start | bytes 772
  32.0 24.2 %collective-permute-start.1 = (bf16[2,64,4096]{2,1,0:T(8,128)(2,1)S(1)}, bf16[2,64,4096]{2,1,0:T(8,128)(2,1)S(1)}, u32[]{:S(2)}, u32[]{:S(2)}) collective-permute-start(bf16[2,64,4096]{2,1,0:T(8,128)(2,1)S(1)} %maximum_select_fusion.1), channel_id=1, source_target_pairs={{0,8},{4,12},{8,0},{12,4},{16,24},{20,28},{24,16},{28,20},{1,9},{5... | collective-permute-start | bytes 3145736 | tf_op jit(solution)/shard_map/ppermute | solution.py:14
  32.7 53.5 %copy-start.5 = (f32[2,4096]{1,0:T(2,128)}, f32[2,4096]{1,0:T(2,128)S(1)}, u32[]{:S(2)}) copy-start(f32[2,4096]{1,0:T(2,128)S(1)} %get-tuple-element.16) | copy-start | bytes 98308
  32.7 53.5 %copy-start.7 = (f32[2,4096]{1,0:T(2,128)}, f32[2,4096]{1,0:T(2,128)S(1)}, u32[]{:S(2)}) copy-start(f32[2,4096]{1,0:T(2,128)S(1)} %get-tuple-element.17) | copy-start | bytes 98308
  56.2 30.0 %copy-start.2 = (bf16[2,64,4096]{2,1,0:T(8,128)(2,1)}, bf16[2,64,4096]{2,1,0:T(8,128)(2,1)S(1)}, u32[]{:S(2)}) copy-start(bf16[2,64,4096]{2,1,0:T(8,128)(2,1)S(1)} %collective-permute-done.1) | copy-start | bytes 3145732
  56.9 29.2 %copy-start.9 = (f32[2,128]{1,0:T(2,128)}, f32[2,128]{1,0:T(2,128)S(1)}, u32[]{:S(2)}) copy-start(f32[2,128]{1,0:T(2,128)S(1)} %add_rsqrt_fusion) | copy-start | bytes 3076
  56.9 14.7 %copy-start.13 = (bf16[1,2,4096,32]{2,3,1,0:T(8,128)(2,1)S(1)}, bf16[1,2,4096,32]{2,3,1,0:T(8,128)(2,1)}, u32[]{:S(2)}) copy-start(bf16[1,2,4096,32]{2,3,1,0:T(8,128)(2,1)} %param.15) | copy-start | bytes 1572868
  71.7 14.5 %copy-start.1 = (bf16[1,2,4096,128]{3,2,1,0:T(8,128)(2,1)S(1)}, bf16[1,2,4096,128]{3,2,1,0:T(8,128)(2,1)}, u32[]{:S(2)}) copy-start(bf16[1,2,4096,128]{3,2,1,0:T(8,128)(2,1)} %param.13) | copy-start | bytes 6291460
  89.4 40.0 %reduce-scatter.4.cloned.1.call-start = ((), (), s32[]{:S(2)}) async-start(), calls=%async_computation.3 | async-start | bytes 163840 | tf_op jit(solution)/shard_map/reduce_scatter | solution.py:24
  89.6 40.5 %copy-start.6 = (f32[2,4096]{1,0:T(2,128)S(1)}, f32[2,4096]{1,0:T(2,128)}, u32[]{:S(2)}) copy-start(f32[2,4096]{1,0:T(2,128)} %copy-done.5) | copy-start | bytes 98308
  89.6 40.5 %copy-start.8 = (f32[2,4096]{1,0:T(2,128)S(1)}, f32[2,4096]{1,0:T(2,128)}, u32[]{:S(2)}) copy-start(f32[2,4096]{1,0:T(2,128)} %copy-done.7) | copy-start | bytes 98308
  91.5 120.5 %reduce-scatter.8.cloned.1.call-start = ((), (), s32[]{:S(2)}) async-start(), calls=%async_computation.5 | async-start | bytes 1310720 | tf_op jit(solution)/shard_map/reduce_scatter | solution.py:24
  135.9 45.1 %collective-permute-start.6 = (f32[2,64,4096]{2,1,0:T(8,128)S(1)}, f32[2,64,4096]{2,1,0:T(8,128)S(1)}, u32[]{:S(2)}, u32[]{:S(2)}) collective-permute-start(f32[2,64,4096]{2,1,0:T(8,128)S(1)} %slice_select_fusion), channel_id=1, source_target_pairs={{0,8},{4,12},{8,0},{12,4},{16,24},{20,28},{24,16},{28,20},{1,9},{5... | collective-permute-start | bytes 6291464 | tf_op jit(solution)/shard_map/ppermute | solution.py:14
  181.6 5.5 %copy-start.14 = (u32[32]{0:T(128)S(1)}, u32[32]{0:T(128)}, u32[]{:S(2)}) copy-start(u32[32]{0:T(128)} %constant.90) | copy-start | bytes 388
  181.6 7.8 %copy-start.10 = (f32[2,128]{1,0:T(2,128)S(1)}, f32[2,128]{1,0:T(2,128)}, u32[]{:S(2)}) copy-start(f32[2,128]{1,0:T(2,128)} %copy-done.9) | copy-start | bytes 3076
  181.6 30.4 %copy-start.3 = (bf16[1,2,32,1024]{3,2,1,0:T(8,128)(2,1)S(1)}, bf16[1,2,32,1024]{3,2,1,0:T(8,128)(2,1)}, u32[]{:S(2)}) copy-start(bf16[1,2,32,1024]{3,2,1,0:T(8,128)(2,1)} %param.8) | copy-start | bytes 393220
  181.6 30.4 %copy-start.4 = (bf16[1,2,32,1024]{3,2,1,0:T(8,128)(2,1)S(1)}, bf16[1,2,32,1024]{3,2,1,0:T(8,128)(2,1)}, u32[]{:S(2)}) copy-start(bf16[1,2,32,1024]{3,2,1,0:T(8,128)(2,1)} %param.9) | copy-start | bytes 393220
  181.6 2.7 %collective-permute-start.7 = (f32[2,32,4096]{2,1,0:T(8,128)S(1)}, f32[2,32,4096]{2,1,0:T(8,128)S(1)}, u32[]{:S(2)}, u32[]{:S(2)}) collective-permute-start(f32[2,32,4096]{2,1,0:T(8,128)S(1)} %slice_select_fusion.1), channel_id=1, source_target_pairs={{0,4},{4,0},{8,12},{12,8},{16,20},{20,16},{24,28},{28,24},{1,5},{5... | collective-permute-start | bytes 3145736 | tf_op jit(solution)/shard_map/ppermute | solution.py:14
  185.6 3.6 %collective-permute-start.8 = (f32[2,64,4]{1,0,2:T(2,128)S(1)}, f32[2,64,4]{1,0,2:T(2,128)S(1)}, u32[]{:S(2)}, u32[]{:S(2)}) collective-permute-start(f32[2,64,4]{1,0,2:T(2,128)S(1)} %broadcast_in_dim.67), channel_id=1, source_target_pairs={{0,8},{4,12},{8,0},{12,4},{16,24},{20,28},{24,16},{28,20},{1,9},{5... | collective-permute-start | bytes 6152 | tf_op jit(solution)/shard_map/ppermute | solution.py:14
  189.3 1.2 collective-permute-start.9
  213.2 5.0 %collective-permute-start.10 = (bf16[2,32,1024]{2,1,0:T(8,128)(2,1)S(1)}, bf16[2,32,1024]{2,1,0:T(8,128)(2,1)S(1)}, u32[]{:S(2)}, u32[]{:S(2)}) collective-permute-start(bf16[2,32,1024]{2,1,0:T(8,128)(2,1)S(1)} %fusion.32), channel_id=1, source_target_pairs={{0,16},{4,20},{8,24},{12,28},{16,0},{20,4},{24,8},{28,12},{1,17},{... | collective-permute-start | bytes 393224 | tf_op jit(solution)/shard_map/ppermute | solution.py:19
Sparse Core Ops, SparseCore 0:
  89.5 19.9 reduce-scatter.5
  111.7 17.5 reduce-scatter.3
  185.7 26.2 reduce-scatter.7
where the time goes:
time: 226 us; the launch traced here: 225 us
  waiting for transfers between devices  123 us (54%)
  blocking collectives  54.3 us (24%)
  matrix products  13.8 us (6%)
  between operations  13.4 us (6%)
  other arithmetic  9.83 us (4%)
  starting transfers between devices  7.91 us (4%)
  local copies, waits for them, and re-layouts  3.58 us (2%)
    ppermute x10, waiting for transfers between devices, swapped(): return lax.ppermute(value, axis, pairs)  75.4 us
    reduce_scatter x2, waiting for transfers between devices, sum_columns(): lax.psum_scatter(first, 'tensor', scatter_dimension=2, tiled=True)  29.9 us
    all_gather x1, blocking collectives, per_device(): x_cols = lax.all_gather(x_local, 'tensor', axis=2, tiled=True)  17.7 us
    reduce_scatter x1, waiting for transfers between devices, sum_columns(): lax.psum_scatter(second, 'tensor', scatter_dimension=2, tiled=True)  13.9 us
    all_gather x1, blocking collectives, per_device(): lax.all_gather(key_part, 'tensor', axis=2, tiled=True)  13.4 us
    all_gather x1, blocking collectives, per_device(): lax.all_gather(value_part, 'tensor', axis=2, tiled=True)  13.2 us
    unnamed x1, blocking collectives  10 us
    ppermute x10, starting transfers between devices, swapped(): return lax.ppermute(value, axis, pairs)  6.29 us
  transfers between devices with their start and end apart: 14, of which 11 were waited for; matrix products, arithmetic and copies ran while one was open for 4% of the time, Pallas kernels for 0%

commit v1 on v0

--- a/solution.py
+++ b/solution.py
@@ -67,7 +67,23 @@
     w_query = w_query[0]
     w_key = w_key[0]
     w_value = w_value[0]
-    x_cols = lax.all_gather(x_local, "tensor", axis=2, tiled=True)
+    size, index, rows = (lax.axis_size("tensor"), lax.axis_index("tensor"), x_local.shape[2])
+    right = [(i_2, (i_2 + 1) % size) for i_2 in range(size)]
+    left = [(i_2, (i_2 - 1) % size) for i_2 in range(size)]
+    x_cols = jnp.zeros((*x_local.shape[:2], size * rows, *x_local.shape[2 + 1 :]), x_local.dtype)
+    x_cols = lax.dynamic_update_slice_in_dim(x_cols, x_local, index * rows, axis=2)
+    from_left = from_right = x_local
+    half = size // 2
+    for step in range(1, half + 1):
+        from_left = lax.ppermute(from_left, "tensor", right)
+        x_cols = lax.dynamic_update_slice_in_dim(
+            x_cols, from_left, (index - step) % size * rows, axis=2
+        )
+        if step < size - half:
+            from_right = lax.ppermute(from_right, "tensor", left)
+            x_cols = lax.dynamic_update_slice_in_dim(
+                x_cols, from_right, (index + step) % size * rows, axis=2
+            )
     x_full = collect_rows(x_cols, position, levels, 1)
     kind_full = collect_rows(types[0].astype(jnp.bfloat16), position, levels, 1)
     gain_full = collect_rows(gains[0], position, levels, 2).astype(jnp.float32)

time: 226 us -> 219 us (0.969)
  blocking collectives: 54.3 us -> 36.3 us
  starting transfers between devices: 7.91 us -> 14.2 us
  waiting for transfers between devices: 123 us -> 126 us
    all_gather x1 -> x0, blocking collectives: 17.7 us -> none  [per_device(): x_cols = lax.all_gather(x_local, 'tensor', axis=2, tiled=True)]
    ppermute x0 -> x3, waiting for transfers between devices: none -> 6.8 us  [the longest x2 6.12 us: per_device(): from_left = lax.ppermute(from_left, 'tensor', right)]
    ppermute x0 -> x3, starting transfers between devices: none -> 5.08 us  [the longest x2 3.05 us: per_device(): from_left = lax.ppermute(from_left, 'tensor', right)]
  transfers between devices with their start and end apart: 14 -> 17, of which waited for: 11 -> 12; matrix products, arithmetic and copies ran while one was open for 4% -> 5% of each run, Pallas kernels for 0% -> 0%
where the time goes in v1:
time: 219 us; the launch traced here: 218 us
  waiting for transfers between devices  126 us (58%)
  blocking collectives  36.3 us (17%)
  starting transfers between devices  14.2 us (6%)
  matrix products  13.7 us (6%)
  between operations  13.4 us (6%)
  other arithmetic  9.78 us (4%)
  local copies, waits for them, and re-layouts  4.61 us (2%)
    ppermute x10, waiting for transfers between devices, swapped(): return lax.ppermute(value, axis, pairs)  74 us
    reduce_scatter x2, waiting for transfers between devices, sum_columns(): lax.psum_scatter(first, 'tensor', scatter_dimension=2, tiled=True)  29.9 us
    all_gather x1, blocking collectives, per_device(): lax.all_gather(key_part, 'tensor', axis=2, tiled=True)  13.1 us
    all_gather x1, blocking collectives, per_device(): lax.all_gather(value_part, 'tensor', axis=2, tiled=True)  13.1 us
    reduce_scatter x1, waiting for transfers between devices, sum_columns(): lax.psum_scatter(second, 'tensor', scatter_dimension=2, tiled=True)  12.3 us
    unnamed x1, blocking collectives  10 us
    ppermute x10, starting transfers between devices, swapped(): return lax.ppermute(value, axis, pairs)  7.45 us
    ppermute x2, waiting for transfers between devices, per_device(): from_left = lax.ppermute(from_left, 'tensor', right)  6.12 us
  transfers between devices with their start and end apart: 17, of which 12 were waited for; matrix products, arithmetic and copies ran while one was open for 5% of the time, Pallas kernels for 0%

profile of v1, /device:TPU:0, one launch (start us, length us, event | category | flops | bytes accessed | tf_op | source)
XLA Modules:
  0.0 218.4 jit_solution(9109123076796079554)
XLA Ops:
  6.5 3.1 %collective-permute-start = (bf16[2,32,1024]{2,1,0:T(8,128)(2,1)}, bf16[2,32,1024]{2,1,0:T(8,128)(2,1)S(1)}, u32[]{:S(2)}, u32[]{:S(2)}) collective-permute-start(bf16[2,32,1024]{2,1,0:T(8,128)(2,1)} %bitcast.52), channel_id=1, source_target_pairs={{0,1},{1,2},{2,3},{3,0},{4,5},{5,6},{6,7},{7,4},{8,9},{9,10},{10,1... | collective-permute-start | bytes 393224 | tf_op jit(solution)/shard_map/ppermute | solution.py:78
  9.6 2.0 collective-permute-start.1
  11.6 0.7 convert_bitcast_fusion
  12.3 0.5 collective-permute-start.7
  12.9 1.0 constant_dynamic-update-slice_fusion.3
  14.0 1.7 collective-permute-start.6
  15.7 0.8 broadcast_select_fusion.2
  16.5 0.4 collective-permute-start.8
  16.9 0.7 collective-permute-done.1
  17.6 6.1 %collective-permute-done.2 = bf16[2,32,1024]{2,1,0:T(8,128)(2,1)S(1)} collective-permute-done((bf16[2,32,1024]{2,1,0:T(8,128)(2,1)S(1)}, bf16[2,32,1024]{2,1,0:T(8,128)(2,1)S(1)}, u32[]{:S(2)}, u32[]{:S(2)}) %collective-permute-start.2) | collective-permute-done | bytes 131104 | tf_op jit(solution)/shard_map/ppermute | solution.py:78
  23.9 1.8 collective-permute-done.3
  25.9 1.7 collective-permute-start.4
  27.7 23.4 %collective-permute-done.4 = bf16[2,64,4096]{2,1,0:T(8,128)(2,1)S(1)} collective-permute-done((bf16[2,64,4096]{2,1,0:T(8,128)(2,1)S(1)}, bf16[2,64,4096]{2,1,0:T(8,128)(2,1)S(1)}, u32[]{:S(2)}, u32[]{:S(2)}) %collective-permute-start.4) | collective-permute-done | bytes 1048608 | tf_op jit(solution)/shard_map/ppermute | solution.py:14
  51.2 0.8 fusion.2
  52.0 1.3 convolution_convert_fusion.2
  53.2 13.1 %all_gather.6 = bf16[2,128,128]{1,2,0:T(8,128)(2,1)S(1)} all-gather(bf16[2,128,32]{1,2,0:T(8,128)(2,1)S(1)} %convolution_convert_fusion.2), channel_id=1, replica_groups=mesh['section'=8,'tensor'=4] {'tensor'}, dimensions={2}, use_global_device_ids=true | all-gather | bytes 81920 | tf_op jit(solution)/shard_map/all_gather | solution.py:108
  66.4 1.3 convolution_convert_fusion.1
  67.7 13.1 %all_gather.7 = bf16[2,128,128]{1,2,0:T(8,128)(2,1)S(1)} all-gather(bf16[2,128,32]{1,2,0:T(8,128)(2,1)S(1)} %convolution_convert_fusion.1), channel_id=1, replica_groups=mesh['section'=8,'tensor'=4] {'tensor'}, dimensions={2}, use_global_device_ids=true | all-gather | bytes 81920 | tf_op jit(solution)/shard_map/all_gather | solution.py:109
  80.8 1.4 fusion.22
  82.2 0.2 fusion.18
  82.4 0.7 fusion.58
  83.1 0.9 fusion.40
  84.1 0.2 convolution_bitcast_fusion
  84.3 1.9 fusion.25
  86.2 2.8 %copy.11 = bf16[1,2,4096,128]{2,3,1,0:T(8,128)(2,1)} copy(bf16[1,2,4096,128]{3,2,1,0:T(8,128)(2,1)S(1)} %copy-done.1) | data formatting | bytes 4194304 | tf_op args[5]
  89.0 1.2 convolution_convert_fusion
  90.2 12.3 %reduce-scatter.6.cloned.1.call-done = f32[2,128,32]{1,2,0:T(8,128)} async-done(((f32[2,128,128]{1,2,0:T(8,128)}), f32[2,128,32]{1,2,0:T(8,128)}) %reduce-scatter.6.cloned.1.call-update) | async-done | bytes 32784 | tf_op jit(solution)/shard_map/reduce_scatter | solution.py:25
  102.5 0.8 convert_element_type.65
  103.2 19.1 %reduce-scatter.4.cloned.1.call-done = f32[2,128,32]{1,2,0:T(8,128)} async-done(((f32[2,128,128]{1,2,0:T(8,128)}), f32[2,128,32]{1,2,0:T(8,128)}) %reduce-scatter.4.cloned.1.call-update) | async-done | bytes 32784 | tf_op jit(solution)/shard_map/reduce_scatter | solution.py:24
  122.3 0.8 convert_element_type.63
  123.1 5.5 %fusion.6 = (f32[2,128]{1,0:T(2,128)S(1)}, f32[2,128,4096]{2,1,0:T(8,128)}, f32[2,128,4096]{2,1,0:T(8,128)S(1)}) fusion(f32[2,4096]{1,0:T(2,128)S(1)} %copy-done.6, f32[2,4096]{1,0:T(2,128)S(1)} %copy-done.8, pred[2,128]{1,0:T(4,128)(4,1)} %copy-done.11, bf16[2,64,4096]{2,1,0:T(8,128)(2,1)} %copy-done.2, bf16[2,64,4096]{2,1,0:T(8,128)(2,1)S(1)} %maximum_select_fusion.1, ...), kind=kOutput, calls=%fused_computation.9 | convolution fusion | flops 427065088 | bytes 13796609 | tf_op jit(solution)/shard_map/cth,cdh->ctd/dot_general | solution.py:140
  128.6 0.3 slice_select_fusion
  128.9 1.5 collective-permute-start.9
  130.4 43.5 %collective-permute-done.9 = f32[2,64,4096]{2,1,0:T(8,128)S(1)} collective-permute-done((f32[2,64,4096]{2,1,0:T(8,128)S(1)}, f32[2,64,4096]{2,1,0:T(8,128)S(1)}, u32[]{:S(2)}, u32[]{:S(2)}) %collective-permute-start.9) | collective-permute-done | bytes 2097184 | tf_op jit(solution)/shard_map/ppermute | solution.py:14
  173.9 0.4 select_add_fusion
  174.6 2.6 %collective-permute-done.10 = f32[2,32,4096]{2,1,0:T(8,128)S(1)} collective-permute-done((f32[2,32,4096]{2,1,0:T(8,128)S(1)}, f32[2,32,4096]{2,1,0:T(8,128)S(1)}, u32[]{:S(2)}, u32[]{:S(2)}) %collective-permute-start.10) | collective-permute-done | bytes 1048608 | tf_op jit(solution)/shard_map/ppermute | solution.py:14
  177.3 1.2 select_add_fusion.1
  178.6 1.5 collective-permute-start.11
  180.0 0.6 dynamic-slice.4
  180.6 1.6 collective-permute-done.11
  182.4 1.1 collective-permute-done.12
  183.5 10.0 %all-reduce = f32[2,32,4]{1,0,2:T(2,128)S(1)} all-reduce(f32[2,32,4]{1,0,2:T(2,128)S(1)} %select_add_fusion.2), channel_id=5, replica_groups=mesh['section'=8,'tensor'=4] {'tensor'}, use_global_device_ids=true, to_apply=%region_8.9.clone | all-reduce | flops 256 | bytes 2048
  193.5 0.7 fusion.48
  194.2 10.8 %reduce-scatter.8.cloned.1.call-done = f32[2,32,1024]{2,1,0:T(8,128)} async-done(((f32[2,32,4096]{2,1,0:T(8,128)}), f32[2,32,1024]{2,1,0:T(8,128)}) %reduce-scatter.8.cloned.1.call-update) | async-done | bytes 262160 | tf_op jit(solution)/shard_map/reduce_scatter | solution.py:24
  204.9 1.2 fusion.29
  206.2 1.6 collective-permute-start.13
  207.8 3.4 %collective-permute-done.13 = bf16[2,32,1024]{2,1,0:T(8,128)(2,1)S(1)} collective-permute-done((bf16[2,32,1024]{2,1,0:T(8,128)(2,1)S(1)}, bf16[2,32,1024]{2,1,0:T(8,128)(2,1)S(1)}, u32[]{:S(2)}, u32[]{:S(2)}) %collective-permute-start.13) | collective-permute-done | bytes 131104 | tf_op jit(solution)/shard_map/ppermute | solution.py:19
  211.2 0.7 fusion.34
  (66 shorter events, 1.4 us)
Async XLA Ops:
  6.5 76.6 %copy-start = (bf16[1,2,128,128]{3,2,1,0:T(8,128)(2,1)S(1)}, bf16[1,2,128,128]{3,2,1,0:T(8,128)(2,1)}, u32[]{:S(2)}) copy-start(bf16[1,2,128,128]{3,2,1,0:T(8,128)(2,1)} %param.10) | copy-start | bytes 196612
  6.5 95.9 %reduce-scatter.6.cloned.1.call-start = ((), (), s32[]{:S(2)}) async-start(), calls=%async_computation.4 | async-start | bytes 163840 | tf_op jit(solution)/shard_map/reduce_scatter | solution.py:25
  6.5 10.3 %collective-permute-start = (bf16[2,32,1024]{2,1,0:T(8,128)(2,1)}, bf16[2,32,1024]{2,1,0:T(8,128)(2,1)S(1)}, u32[]{:S(2)}, u32[]{:S(2)}) collective-permute-start(bf16[2,32,1024]{2,1,0:T(8,128)(2,1)} %bitcast.52), channel_id=1, source_target_pairs={{0,1},{1,2},{2,3},{3,0},{4,5},{5,6},{6,7},{7,4},{8,9},{9,10},{10,1... | collective-permute-start | bytes 393224 | tf_op jit(solution)/shard_map/ppermute | solution.py:78
  9.6 8.0 %collective-permute-start.1 = (bf16[2,32,1024]{2,1,0:T(8,128)(2,1)}, bf16[2,32,1024]{2,1,0:T(8,128)(2,1)S(1)}, u32[]{:S(2)}, u32[]{:S(2)}) collective-permute-start(bf16[2,32,1024]{2,1,0:T(8,128)(2,1)} %bitcast.53), channel_id=1, source_target_pairs={{0,3},{1,0},{2,1},{3,2},{4,7},{5,4},{6,5},{7,6},{8,11},{9,8},{10,9... | collective-permute-start | bytes 393224 | tf_op jit(solution)/shard_map/ppermute | solution.py:83
  12.3 1.6 collective-permute-start.5
  12.3 3.4 %collective-permute-start.7 = (bf16[2,2,1024]{2,1,0:T(2,128)(2,1)}, bf16[2,2,1024]{2,1,0:T(2,128)(2,1)S(1)}, u32[]{:S(2)}, u32[]{:S(2)}) collective-permute-start(bf16[2,2,1024]{2,1,0:T(2,128)(2,1)} %bitcast.57), channel_id=1, source_target_pairs={{0,4},{4,0},{8,12},{12,8},{16,20},{20,16},{24,28},{28,24},{1,5},{5... | collective-permute-start | bytes 24584 | tf_op jit(solution)/shard_map/ppermute | solution.py:14
  12.8 39.1 %copy-start.12 = (bf16[1,2,4096,32]{2,3,1,0:T(8,128)(2,1)S(1)}, bf16[1,2,4096,32]{2,3,1,0:T(8,128)(2,1)}, u32[]{:S(2)}) copy-start(bf16[1,2,4096,32]{2,3,1,0:T(8,128)(2,1)} %param.14) | copy-start | bytes 1572868
  14.0 9.8 %collective-permute-start.6 = (bf16[2,64]{1,0:T(2,128)(2,1)S(1)}, bf16[2,64]{1,0:T(2,128)(2,1)S(1)}, u32[]{:S(2)}, u32[]{:S(2)}) collective-permute-start(bf16[2,64]{1,0:T(2,128)(2,1)S(1)} %broadcast_select_fusion.6), channel_id=1, source_target_pairs={{0,8},{4,12},{8,0},{12,4},{16,24},{20,28},{24,16},{28,20},{1,9},{5... | collective-permute-start | bytes 776 | tf_op jit(solution)/shard_map/ppermute | solution.py:14
  16.5 7.4 %collective-permute-start.8 = (bf16[2,2,2048]{2,1,0:T(2,128)(2,1)S(1)}, bf16[2,2,2048]{2,1,0:T(2,128)(2,1)S(1)}, u32[]{:S(2)}, u32[]{:S(2)}) collective-permute-start(bf16[2,2,2048]{2,1,0:T(2,128)(2,1)S(1)} %broadcast_select_fusion.2), channel_id=1, source_target_pairs={{0,8},{4,12},{8,0},{12,4},{16,24},{20,28},{24,16},{28,20},{1,9},{5... | collective-permute-start | bytes 49160 | tf_op jit(solution)/shard_map/ppermute | solution.py:14
  16.9 6.8 %collective-permute-start.2 = (bf16[2,32,1024]{2,1,0:T(8,128)(2,1)S(1)}, bf16[2,32,1024]{2,1,0:T(8,128)(2,1)S(1)}, u32[]{:S(2)}, u32[]{:S(2)}) collective-permute-start(bf16[2,32,1024]{2,1,0:T(8,128)(2,1)S(1)} %collective-permute-done), channel_id=1, source_target_pairs={{0,1},{1,2},{2,3},{3,0},{4,5},{5,6},{6,7},{7,4},{8,9},{9,10},{10,1... | collective-permute-start | bytes 393224 | tf_op jit(solution)/shard_map/ppermute | solution.py:78
  23.7 2.0 collective-permute-start.3
  23.9 56.9 %copy-start.11 = (pred[2,128]{1,0:T(4,128)(4,1)}, pred[2,128]{1,0:T(4,128)(4,1)S(1)}, u32[]{:S(2)}) copy-start(pred[2,128]{1,0:T(4,128)(4,1)S(1)} %fusion.49) | copy-start | bytes 772
  25.9 25.3 %collective-permute-start.4 = (bf16[2,64,4096]{2,1,0:T(8,128)(2,1)S(1)}, bf16[2,64,4096]{2,1,0:T(8,128)(2,1)S(1)}, u32[]{:S(2)}, u32[]{:S(2)}) collective-permute-start(bf16[2,64,4096]{2,1,0:T(8,128)(2,1)S(1)} %maximum_select_fusion.1), channel_id=1, source_target_pairs={{0,8},{4,12},{8,0},{12,4},{16,24},{20,28},{24,16},{28,20},{1,9},{5... | collective-permute-start | bytes 3145736 | tf_op jit(solution)/shard_map/ppermute | solution.py:14
  27.7 53.1 %copy-start.5 = (f32[2,4096]{1,0:T(2,128)}, f32[2,4096]{1,0:T(2,128)S(1)}, u32[]{:S(2)}) copy-start(f32[2,4096]{1,0:T(2,128)S(1)} %get-tuple-element.16) | copy-start | bytes 98308
  27.7 53.0 %copy-start.7 = (f32[2,4096]{1,0:T(2,128)}, f32[2,4096]{1,0:T(2,128)S(1)}, u32[]{:S(2)}) copy-start(f32[2,4096]{1,0:T(2,128)S(1)} %get-tuple-element.17) | copy-start | bytes 98308
  51.2 29.6 %copy-start.2 = (bf16[2,64,4096]{2,1,0:T(8,128)(2,1)}, bf16[2,64,4096]{2,1,0:T(8,128)(2,1)S(1)}, u32[]{:S(2)}) copy-start(bf16[2,64,4096]{2,1,0:T(8,128)(2,1)S(1)} %collective-permute-done.4) | copy-start | bytes 3145732
  51.9 28.9 %copy-start.9 = (f32[2,128]{1,0:T(2,128)}, f32[2,128]{1,0:T(2,128)S(1)}, u32[]{:S(2)}) copy-start(f32[2,128]{1,0:T(2,128)S(1)} %add_rsqrt_fusion) | copy-start | bytes 3076
  52.0 14.4 %copy-start.13 = (bf16[1,2,4096,32]{2,3,1,0:T(8,128)(2,1)S(1)}, bf16[1,2,4096,32]{2,3,1,0:T(8,128)(2,1)}, u32[]{:S(2)}) copy-start(bf16[1,2,4096,32]{2,3,1,0:T(8,128)(2,1)} %param.15) | copy-start | bytes 1572868
  66.4 14.4 %copy-start.1 = (bf16[1,2,4096,128]{3,2,1,0:T(8,128)(2,1)S(1)}, bf16[1,2,4096,128]{3,2,1,0:T(8,128)(2,1)}, u32[]{:S(2)}) copy-start(bf16[1,2,4096,128]{3,2,1,0:T(8,128)(2,1)} %param.13) | copy-start | bytes 6291460
  84.0 38.3 %reduce-scatter.4.cloned.1.call-start = ((), (), s32[]{:S(2)}) async-start(), calls=%async_computation.3 | async-start | bytes 163840 | tf_op jit(solution)/shard_map/reduce_scatter | solution.py:24
  84.3 38.8 %copy-start.6 = (f32[2,4096]{1,0:T(2,128)S(1)}, f32[2,4096]{1,0:T(2,128)}, u32[]{:S(2)}) copy-start(f32[2,4096]{1,0:T(2,128)} %copy-done.5) | copy-start | bytes 98308
  84.3 38.8 %copy-start.8 = (f32[2,4096]{1,0:T(2,128)S(1)}, f32[2,4096]{1,0:T(2,128)}, u32[]{:S(2)}) copy-start(f32[2,4096]{1,0:T(2,128)} %copy-done.7) | copy-start | bytes 98308
  86.2 118.8 %reduce-scatter.8.cloned.1.call-start = ((), (), s32[]{:S(2)}) async-start(), calls=%async_computation.5 | async-start | bytes 1310720 | tf_op jit(solution)/shard_map/reduce_scatter | solution.py:24
  128.9 45.0 %collective-permute-start.9 = (f32[2,64,4096]{2,1,0:T(8,128)S(1)}, f32[2,64,4096]{2,1,0:T(8,128)S(1)}, u32[]{:S(2)}, u32[]{:S(2)}) collective-permute-start(f32[2,64,4096]{2,1,0:T(8,128)S(1)} %slice_select_fusion), channel_id=1, source_target_pairs={{0,8},{4,12},{8,0},{12,4},{16,24},{20,28},{24,16},{28,20},{1,9},{5... | collective-permute-start | bytes 6291464 | tf_op jit(solution)/shard_map/ppermute | solution.py:14
  174.5 5.6 %copy-start.14 = (u32[32]{0:T(128)S(1)}, u32[32]{0:T(128)}, u32[]{:S(2)}) copy-start(u32[32]{0:T(128)} %constant.108) | copy-start | bytes 388
  174.5 7.8 %copy-start.10 = (f32[2,128]{1,0:T(2,128)S(1)}, f32[2,128]{1,0:T(2,128)}, u32[]{:S(2)}) copy-start(f32[2,128]{1,0:T(2,128)} %copy-done.9) | copy-start | bytes 3076
  174.5 30.4 %copy-start.3 = (bf16[1,2,32,1024]{3,2,1,0:T(8,128)(2,1)S(1)}, bf16[1,2,32,1024]{3,2,1,0:T(8,128)(2,1)}, u32[]{:S(2)}) copy-start(bf16[1,2,32,1024]{3,2,1,0:T(8,128)(2,1)} %param.8) | copy-start | bytes 393220
  174.5 30.4 %copy-start.4 = (bf16[1,2,32,1024]{3,2,1,0:T(8,128)(2,1)S(1)}, bf16[1,2,32,1024]{3,2,1,0:T(8,128)(2,1)}, u32[]{:S(2)}) copy-start(bf16[1,2,32,1024]{3,2,1,0:T(8,128)(2,1)} %param.9) | copy-start | bytes 393220
  174.5 2.7 %collective-permute-start.10 = (f32[2,32,4096]{2,1,0:T(8,128)S(1)}, f32[2,32,4096]{2,1,0:T(8,128)S(1)}, u32[]{:S(2)}, u32[]{:S(2)}) collective-permute-start(f32[2,32,4096]{2,1,0:T(8,128)S(1)} %slice_select_fusion.1), channel_id=1, source_target_pairs={{0,4},{4,0},{8,12},{12,8},{16,20},{20,16},{24,28},{28,24},{1,5},{5... | collective-permute-start | bytes 3145736 | tf_op jit(solution)/shard_map/ppermute | solution.py:14
  178.6 3.6 %collective-permute-start.11 = (f32[2,64,4]{1,0,2:T(2,128)S(1)}, f32[2,64,4]{1,0,2:T(2,128)S(1)}, u32[]{:S(2)}, u32[]{:S(2)}) collective-permute-start(f32[2,64,4]{1,0,2:T(2,128)S(1)} %broadcast_in_dim.71), channel_id=1, source_target_pairs={{0,8},{4,12},{8,0},{12,4},{16,24},{20,28},{24,16},{28,20},{1,9},{5... | collective-permute-start | bytes 6152 | tf_op jit(solution)/shard_map/ppermute | solution.py:14
  182.3 1.2 collective-permute-start.12
  206.2 5.0 %collective-permute-start.13 = (bf16[2,32,1024]{2,1,0:T(8,128)(2,1)S(1)}, bf16[2,32,1024]{2,1,0:T(8,128)(2,1)S(1)}, u32[]{:S(2)}, u32[]{:S(2)}) collective-permute-start(bf16[2,32,1024]{2,1,0:T(8,128)(2,1)S(1)} %fusion.29), channel_id=1, source_target_pairs={{0,16},{4,20},{8,24},{12,28},{16,0},{20,4},{24,8},{28,12},{1,17},{... | collective-permute-start | bytes 393224 | tf_op jit(solution)/shard_map/ppermute | solution.py:19
Sparse Core Ops, SparseCore 0:
  84.1 18.2 reduce-scatter.5
  104.7 17.5 reduce-scatter.3
  178.6 26.2 reduce-scatter.7
